TPU v7x, 128 devices: a whole 4x4x4 slice. The times are simulated.
128 devices in a mesh: wide: 16 (over x_hi, z, core), narrow: 8 (over y, x_lo).
Axes of the slice: x: 4 (x_hi: 2, x_lo: 2; x = x_hi * 2 + x_lo), y: 4, z: 4, core: 2. Of those that a mesh axis runs over, the one named last changes fastest.
Arguments:
- block_states: bfloat16 [32, 64, 4096], P('wide', None, 'narrow'), may hold values from -6 to 6
- attn_gain: float32 [4096], replicated, may hold values from 0.1 to 1.9
- ffn_gain: float32 [4096], replicated, may hold values from 0.1 to 1.9
- final_gain: float32 [4096], replicated, may hold values from 0.1 to 1.9
- w_query: bfloat16 [4096, 4096], P(None, 'narrow'), may hold values from -0.09375 to 0.09375
- w_keyval: bfloat16 [4096, 1024], replicated, may hold values from -0.09375 to 0.09375
- w_out: bfloat16 [4096, 4096], P('narrow'), may hold values from -0.09375 to 0.09375
- w_gate: bfloat16 [4096, 1024], P(None, 'narrow'), may hold values from -0.09375 to 0.09375
- w_up: bfloat16 [4096, 1024], P(None, 'narrow'), may hold values from -0.09375 to 0.09375
- w_down: bfloat16 [1024, 4096], P('narrow'), may hold values from -0.1875 to 0.1875
- w_head: bfloat16 [4096, 131072], P(None, ('wide', 'narrow')), may hold values from -8 to 8
- cache: bfloat16 [32, 512, 4, 256], P('wide'), may hold values from -2000 to 2000
- prefix_lengths: int32 [32], P('wide'), may hold values from 128 to 512, as said below
- masked_positions: int32 [16, 64], replicated, may hold values from 0 to 63, as said below
Outputs:
- log_probs: float32 [1024, 131072], P(None, ('wide', 'narrow'))
- confidence: float32 [16, 64], replicated
Inputs may be any that keep to these rules, and one draw needn't show every extreme that they name: `prefix_lengths`: some request branch has exactly 512 valid positions. `masked_positions`: the 64 positions of one request are distinct.
All inputs are finite; a program needn't handle non-finite values.
Results may differ from a plain program's by a relative error of at most 0.024.
The roundings to bfloat16 on the way count: a program that leaves them out, or rounds other values in their place, can miss the bound.
Values may be sent and summed in bfloat16 or wider, within the bound.
No kernel may reach another device: no remote copies, remote signals or barrier semaphores. Data moves between devices by JAX's collectives and lax.ppermute only.
A program may use at most 128 MiB of HBM per device.

v0:
```python
import math
import jax
import jax.numpy as jnp
from jax import lax
from jax.sharding import PartitionSpec as P

KVH = 4
HD = 128
EPS = 1e-06
GUIDE = 1.5


def swapped(value, axis, bit):
    mask = 2**bit
    pairs = [(source, source ^ mask) for source in range(lax.axis_size(axis))]
    return lax.ppermute(value, axis, pairs)


def rms_scale(rows, gain):
    return rows * lax.rsqrt(jnp.mean(rows * rows, axis=-1, keepdims=True) + EPS) * gain


def split_halves(rows, is_upper, kept_count):
    lower_part = rows[:kept_count]
    upper_part = rows[kept_count:]
    outgoing = jnp.where(is_upper, lower_part, upper_part)
    own_rows = jnp.where(is_upper, upper_part, lower_part)
    return (outgoing, own_rows)


def guide_rows(own_rows, partner, is_upper):
    cond_rows = jnp.where(is_upper, partner, own_rows)
    uncond_rows = jnp.where(is_upper, own_rows, partner)
    return (uncond_rows + GUIDE * (cond_rows - uncond_rows)).astype(jnp.bfloat16)


def on_device(
    block_states,
    attn_gain,
    ffn_gain,
    final_gain,
    w_query,
    w_keyval,
    w_out,
    w_gate,
    w_up,
    w_down,
    w_head,
    cache,
    prefix_lengths,
    masked_positions,
):
    n_wide = lax.axis_size("wide")
    n_narrow = lax.axis_size("narrow")
    wide_index = lax.axis_index("wide")
    narrow_index = lax.axis_index("narrow")
    half_wide = n_wide // 2
    local_req = block_states.shape[0]
    kept_count = local_req // 2
    masked = masked_positions.shape[1]
    is_upper = wide_index >= half_wide
    full_rows = lax.all_gather(block_states, "narrow", axis=2, tiled=True)
    normed = rms_scale(full_rows.astype(jnp.float32), attn_gain).astype(jnp.bfloat16)
    kv_head = narrow_index // (n_narrow // KVH)
    head_weight = lax.dynamic_slice_in_dim(w_keyval, kv_head * (2 * HD), 2 * HD, 1)
    block_kv = jnp.einsum(
        "bld,dc->blc", normed, head_weight, preferred_element_type=jnp.float32
    ).astype(jnp.bfloat16)
    cache_kv = lax.dynamic_index_in_dim(cache, kv_head, axis=2, keepdims=False)
    first_req = wide_index % half_wide * local_req
    my_positions = lax.dynamic_slice_in_dim(masked_positions, first_req, local_req, 0)
    picked = jax.vmap(lambda rows, idx: rows[idx])(full_rows, my_positions)
    picked_normed = jax.vmap(lambda rows, idx: rows[idx])(normed, my_positions)
    local_heads = w_query.shape[1] // HD
    query = jnp.einsum(
        "bmd,dc->bmc", picked_normed, w_query, preferred_element_type=jnp.float32
    ).astype(jnp.bfloat16)
    query = query.reshape(local_req, masked, local_heads, HD)
    scale = 1.0 / math.sqrt(HD)
    pre_scores = (
        jnp.einsum("bmhd,bpd->bhmp", query, cache_kv[..., :HD], preferred_element_type=jnp.float32)
        * scale
    )
    live = jnp.arange(cache_kv.shape[1])[None, :] < prefix_lengths[:, None]
    pre_scores = jnp.where(live[:, None, None, :], pre_scores, -jnp.inf)
    blk_scores = (
        jnp.einsum("bmhd,bld->bhml", query, block_kv[..., :HD], preferred_element_type=jnp.float32)
        * scale
    )
    peak = jnp.maximum(
        jnp.max(pre_scores, axis=-1, keepdims=True), jnp.max(blk_scores, axis=-1, keepdims=True)
    )
    pre_weights = jnp.exp(pre_scores - peak)
    blk_weights = jnp.exp(blk_scores - peak)
    weight_total = jnp.sum(pre_weights, axis=-1, keepdims=True) + jnp.sum(
        blk_weights, axis=-1, keepdims=True
    )
    pre_probs = (pre_weights / weight_total).astype(jnp.bfloat16)
    blk_probs = (blk_weights / weight_total).astype(jnp.bfloat16)
    attended = jnp.einsum(
        "bhmp,bpd->bmhd", pre_probs, cache_kv[..., HD:], preferred_element_type=jnp.float32
    )
    attended = attended + jnp.einsum(
        "bhml,bld->bmhd", blk_probs, block_kv[..., HD:], preferred_element_type=jnp.float32
    )
    attended = attended.astype(jnp.bfloat16).reshape(local_req, masked, local_heads * HD)
    attn_part = jnp.einsum("bmc,cd->bmd", attended, w_out, preferred_element_type=jnp.float32)
    attn_total = lax.psum(attn_part, "narrow")
    first = picked.astype(jnp.float32) + attn_total
    ffn_in = rms_scale(first, ffn_gain).astype(jnp.bfloat16)
    gate_act = jnp.einsum("bmd,dc->bmc", ffn_in, w_gate, preferred_element_type=jnp.float32)
    up_act = jnp.einsum("bmd,dc->bmc", ffn_in, w_up, preferred_element_type=jnp.float32)
    hidden = (jax.nn.silu(gate_act) * up_act).astype(jnp.bfloat16)
    ffn_part = jnp.einsum("bmc,cd->bmd", hidden, w_down, preferred_element_type=jnp.float32)
    swap_bit = n_wide.bit_length() - 2
    vocab_cols = w_head.shape[1]
    ffn_total = lax.psum(ffn_part, "narrow")
    final = rms_scale(first + ffn_total, final_gain)
    outgoing, own_rows = split_halves(final, is_upper, kept_count)
    partner = swapped(outgoing, "wide", swap_bit)
    guided = guide_rows(own_rows, partner, is_upper).reshape(kept_count * masked, -1)
    logits = jnp.dot(
        lax.all_gather(guided, "wide", axis=0, tiled=True),
        w_head,
        preferred_element_type=jnp.float32,
    )
    logits = logits.reshape(2, half_wide, kept_count, masked, vocab_cols)
    logits = jnp.transpose(logits, (1, 0, 2, 3, 4)).reshape(-1, vocab_cols)
    local_peak = jnp.max(logits, axis=-1)
    row_peak = lax.pmax(local_peak, ("wide", "narrow"))
    row_total = lax.psum(jnp.sum(jnp.exp(logits - row_peak[:, None]), axis=-1), ("wide", "narrow"))
    lse = row_peak + jnp.log(row_total)
    log_probs = logits - lse[:, None]
    confidence = jnp.exp(row_peak - lse).reshape(-1, masked)
    return (log_probs, confidence)


def solution(mesh):
    in_specs = (
        P("wide", None, "narrow"),
        P(),
        P(),
        P(),
        P(None, "narrow"),
        P(),
        P("narrow", None),
        P(None, "narrow"),
        P(None, "narrow"),
        P("narrow", None),
        P(None, ("wide", "narrow")),
        P("wide", None, None, None),
        P("wide"),
        P(),
    )
    out_specs = (P(None, ("wide", "narrow")), P())
    return jax.shard_map(
        on_device, mesh=mesh, in_specs=in_specs, out_specs=out_specs, check_vma=False
    )
```

profile of v0, /device:TPU:1, one launch (start us, length us, event | category | flops | bytes accessed | tf_op | source)
XLA Modules:
  0.0 550.7 jit_solution(10640468757488981066)
XLA Ops:
  10.1 38.0 %all-gather.4.cloned.1.call-done = bf16[2,64,4096]{2,1,0:T(8,128)(2,1)} async-done(((bf16[2,64,512]{2,1,0:T(8,128)(2,1)}), bf16[2,64,4096]{2,1,0:T(8,128)(2,1)}) %all-gather.4.cloned.1.call-update) | async-done | bytes 1048592 | tf_op jit(solution)/shard_map/all_gather | solution.py:62
  48.1 1.5 fusion.6
  49.6 1.6 fusion.8
  51.2 3.9 gather_fusion.1
  55.1 2.2 fusion.23
  61.9 2.1 fusion.2
  65.2 3.9 gather_fusion
  69.1 103.4 %all-reduce.3.cloned.1.call-done = f32[2,64,4096]{2,1,0:T(8,128)} async-done(((f32[2,64,4096]{2,1,0:T(8,128)}), f32[2,64,4096]{2,1,0:T(8,128)}) %all-reduce.3.cloned.1.call-update) | async-done | bytes 2097168 | tf_op jit(solution)/shard_map/psum | solution.py:108
  172.5 2.1 multiply_reduce_fusion.1
  176.1 1.7 fusion.31
  177.8 4.0 fusion.27
  181.8 103.9 %all-reduce.5.cloned.1.call-done = f32[2,64,4096]{2,1,0:T(8,128)} async-done(((f32[2,64,4096]{2,1,0:T(8,128)}), f32[2,64,4096]{2,1,0:T(8,128)}) %all-reduce.5.cloned.1.call-update) | async-done | bytes 2097168 | tf_op jit(solution)/shard_map/psum | solution.py:117
  285.8 2.2 multiply_reduce_fusion
  288.7 2.5 collective-permute-start
  291.2 22.3 %collective-permute-done = f32[1,64,4096]{2,1,0:T(8,128)S(1)} collective-permute-done((f32[1,64,4096]{2,1,0:T(8,128)S(1)}, f32[1,64,4096]{2,1,0:T(8,128)S(1)}, u32[]{:S(2)}, u32[]{:S(2)}) %collective-permute-start) | collective-permute-done | bytes 1048608 | tf_op jit(solution)/shard_map/ppermute | solution.py:16
  314.6 74.8 %all-gather.6.cloned.1.call-done = bf16[1,1024,4096]{2,1,0:T(8,128)(2,1)} async-done(((bf16[1,64,4096]{2,1,0:T(8,128)(2,1)}), bf16[1,1024,4096]{2,1,0:T(8,128)(2,1)}) %all-gather.6.cloned.1.call-update) | async-done | bytes 8388624 | tf_op jit(solution)/shard_map/all_gather | solution.py:123
  389.4 12.6 %fusion = f32[1024,1024]{1,0:T(8,128)S(1)} fusion(bf16[4096,1024]{1,0:T(8,128)(2,1)} %param.24, bf16[1,1024,4096]{2,1,0:T(8,128)(2,1)} %all-gather.6.cloned.1.call-done), kind=kOutput, calls=%fused_computation.2 | convolution fusion | flops 8589934592 | bytes 20971520 | tf_op jit(solution)/shard_map/dot_general | solution.py:122
  402.0 2.0 copy-done.3
  404.0 2.2 copy.39
  406.3 2.5 reduce_max.31
  408.8 64.3 %pmax.7 = f32[1024]{0:T(1024)S(1)} all-reduce(f32[1024]{0:T(1024)S(1)} %reduce_max.32), channel_id=1, replica_groups=mesh['wide'=16,'narrow'=8] {'wide','narrow'}, use_global_device_ids=true, to_apply=%region_10.11 | all-reduce | flops 1024 | bytes 8192 | tf_op jit(solution)/shard_map/pmax | solution.py:130
  473.2 2.9 exponential_reduce_fusion
  476.2 62.5 %psum.23 = f32[1024]{0:T(1024)S(1)} all-reduce(f32[1024]{0:T(1024)S(1)} %reduce_sum.62), channel_id=1, replica_groups=mesh['wide'=16,'narrow'=8] {'wide','narrow'}, use_global_device_ids=true, to_apply=%region_12.13 | all-reduce | flops 1024 | bytes 8192 | tf_op jit(solution)/shard_map/psum | solution.py:131
  539.4 4.7 bitcast_subtract_fusion
  (62 shorter events, 12.9 us)
Async XLA Ops:
  7.2 1.6 copy-start
  7.2 2.8 copy-start.12
  7.2 40.9 %all-gather.4.cloned.1.call-start = ((), (), s32[]{:S(2)}) async-start(), calls=%async_computation | async-start | bytes 1179648 | tf_op jit(solution)/shard_map/all_gather | solution.py:62
  7.9 164.6 %all-reduce.3.cloned.1.call-start = ((), (), s32[]{:S(2)}) async-start(), calls=%async_computation.1 | async-start | bytes 4194304 | tf_op jit(solution)/shard_map/psum | solution.py:108
  8.8 40.8 %copy-start.9 = (f32[4096]{0:T(1024)S(1)}, f32[4096]{0:T(1024)}, u32[]{:S(2)}) copy-start(f32[4096]{0:T(1024)} %param.15) | copy-start | bytes 49156
  55.0 2.8 copy-start.6
  59.7 2.2 copy-start.7
  64.0 1.2 copy-start.2
  64.0 221.7 %all-reduce.5.cloned.1.call-start = ((), (), s32[]{:S(2)}) async-start(), calls=%async_computation.2 | async-start | bytes 4194304 | tf_op jit(solution)/shard_map/psum | solution.py:117
  69.1 105.5 %copy-start.10 = (f32[4096]{0:T(1024)S(1)}, f32[4096]{0:T(1024)}, u32[]{:S(2)}) copy-start(f32[4096]{0:T(1024)} %param.16) | copy-start | bytes 49156
  172.5 2.2 copy-start.4
  174.7 1.4 copy-start.8
  181.8 207.7 %all-gather.6.cloned.1.call-start = ((), (), s32[]{:S(2)}) async-start(), calls=%async_computation.3 | async-start | bytes 8912896 | tf_op jit(solution)/shard_map/all_gather | solution.py:123
  181.8 106.2 %copy-start.11 = (f32[4096]{0:T(1024)S(1)}, f32[4096]{0:T(1024)}, u32[]{:S(2)}) copy-start(f32[4096]{0:T(1024)} %param.17) | copy-start | bytes 49156
  285.8 2.2 copy-start.5
  288.7 24.8 %collective-permute-start = (f32[1,64,4096]{2,1,0:T(8,128)S(1)}, f32[1,64,4096]{2,1,0:T(8,128)S(1)}, u32[]{:S(2)}, u32[]{:S(2)}) collective-permute-start(f32[1,64,4096]{2,1,0:T(8,128)S(1)} %slice_select_fusion), channel_id=1, source_target_pairs={{0,64},{8,72},{16,80},{24,88},{32,96},{40,104},{48,112},{56,120},{... | collective-permute-start | bytes 3145736 | tf_op jit(solution)/shard_map/ppermute | solution.py:16
  402.0 2.0 copy-start.3
  539.4 4.7 copy-start.1
Sparse Core Ops, SparseCore 0:
  9.6 38.3 all-gather.3
  64.1 108.3 all-reduce.2
  181.9 103.8 all-reduce.4
  314.7 74.6 all-gather.5
where the time goes:
time: 551 us
  waiting for transfers between devices  343 us (62%)
  blocking collectives  127 us (23%)
  matrix products  24.6 us (4%)
  other arithmetic  21.8 us (4%)
  local copies, waits for them, and re-layouts  17.4 us (3%)
  between operations  14 us (3%)
    psum x1, waiting for transfers between devices, on_device(): ffn_total = lax.psum(ffn_part, 'narrow')  104 us
    psum x1, waiting for transfers between devices, on_device(): attn_total = lax.psum(attn_part, 'narrow')  103 us
    all_gather x1, waiting for transfers between devices, on_device(): lax.all_gather(guided, 'wide', axis=0, tiled=True)  74.8 us
    pmax x1, blocking collectives, on_device(): row_peak = lax.pmax(local_peak, ('wide', 'narrow'))  64.3 us
    psum x1, blocking collectives, on_device(): lax.psum(jnp.sum(jnp.exp(logits - row_peak[:, None]), axis=-1), ('wide',...  62.5 us
    all_gather x1, waiting for transfers between devices, on_device(): full_rows = lax.all_gather(block_states, 'narrow', axis=2, tiled=True)  38 us
    ppermute x1, waiting for transfers between devices, swapped(): return lax.ppermute(value, axis, pairs)  22.3 us
    dot_general x1, matrix products, on_device(): jnp.dot(lax.all_gather(guided, 'wide', axis=0, tiled=True), w_head, prefe...  12.6 us
  transfers between devices with their start and end apart: 5, of which 5 were waited for; matrix products, arithmetic and copies ran while one was open for 1% of the time, Pallas kernels for 0%

commit v1 on v0

--- a/solution.py
+++ b/solution.py
@@ -105,7 +105,7 @@
     )
     attended = attended.astype(jnp.bfloat16).reshape(local_req, masked, local_heads * HD)
     attn_part = jnp.einsum("bmc,cd->bmd", attended, w_out, preferred_element_type=jnp.float32)
-    attn_total = lax.psum(attn_part, "narrow")
+    attn_total = jnp.sum(lax.all_gather(attn_part, "narrow"), axis=0)
     first = picked.astype(jnp.float32) + attn_total
     ffn_in = rms_scale(first, ffn_gain).astype(jnp.bfloat16)
     gate_act = jnp.einsum("bmd,dc->bmc", ffn_in, w_gate, preferred_element_type=jnp.float32)

time: 551 us -> 779 us (1.41)
  waiting for transfers between devices: 343 us -> 566 us
    all_gather x0 -> x1, waiting for transfers between devices: none -> 325 us  [on_device(): attn_total = jnp.sum(lax.all_gather(attn_part, 'narrow'), axis=0)]
    psum x1 -> x0, waiting for transfers between devices: 103 us -> none  [on_device(): attn_total = lax.psum(attn_part, 'narrow')]
where the time goes in v1:
time: 779 us; the launch traced here: 778 us
  waiting for transfers between devices  566 us (73%)
  blocking collectives  127 us (16%)
  other arithmetic  26.5 us (3%)
  matrix products  23.3 us (3%)
  local copies, waits for them, and re-layouts  18.6 us (2%)
  between operations  14 us (2%)
    all_gather x1, waiting for transfers between devices, on_device(): attn_total = jnp.sum(lax.all_gather(attn_part, 'narrow'), axis=0)  325 us
    psum x1, waiting for transfers between devices, on_device(): ffn_total = lax.psum(ffn_part, 'narrow')  105 us
    all_gather x1, waiting for transfers between devices, on_device(): lax.all_gather(guided, 'wide', axis=0, tiled=True)  74.8 us
    pmax x1, blocking collectives, on_device(): row_peak = lax.pmax(local_peak, ('wide', 'narrow'))  64.1 us
    psum x1, blocking collectives, on_device(): lax.psum(jnp.sum(jnp.exp(logits - row_peak[:, None]), axis=-1), ('wide',...  62.5 us
    all_gather x1, waiting for transfers between devices, on_device(): full_rows = lax.all_gather(block_states, 'narrow', axis=2, tiled=True)  38 us
    ppermute x1, waiting for transfers between devices, swapped(): return lax.ppermute(value, axis, pairs)  22.3 us
  transfers between devices with their start and end apart: 5, of which 5 were waited for; matrix products, arithmetic and copies ran while one was open for 1% of the time, Pallas kernels for 0%

profile of v1, /device:TPU:1, one launch (start us, length us, event | category | flops | bytes accessed | tf_op | source)
XLA Modules:
  0.0 778.1 jit_solution(15127973261680857272)
XLA Ops:
  10.1 38.0 %all-gather.6.cloned.1.call-done = bf16[2,64,4096]{2,1,0:T(8,128)(2,1)} async-done(((bf16[2,64,512]{2,1,0:T(8,128)(2,1)}), bf16[2,64,4096]{2,1,0:T(8,128)(2,1)}) %all-gather.6.cloned.1.call-update) | async-done | bytes 1048592 | tf_op jit(solution)/shard_map/all_gather | solution.py:62
  48.1 1.5 fusion.6
  49.6 1.6 fusion.8
  51.2 3.9 gather_fusion.1
  55.1 2.2 fusion.23
  60.4 1.5 copy-done.7
  61.9 2.1 fusion.2
  65.2 3.9 gather_fusion
  69.1 324.9 %all-gather.8.cloned.1.call-done = f32[16,64,4096]{2,1,0:T(8,128)} async-done(((f32[2,64,4096]{2,1,0:T(8,128)}), f32[16,64,4096]{2,1,0:T(8,128)}) %all-gather.8.cloned.1.call-update) | async-done | bytes 16777232 | tf_op jit(solution)/shard_map/all_gather | solution.py:108
  394.0 7.4 reduce_sum.68
  404.0 4.0 fusion.27
  408.1 105.1 %all-reduce.2.cloned.1.call-done = f32[2,64,4096]{2,1,0:T(8,128)} async-done(((f32[2,64,4096]{2,1,0:T(8,128)}), f32[2,64,4096]{2,1,0:T(8,128)}) %all-reduce.2.cloned.1.call-update) | async-done | bytes 2097168 | tf_op jit(solution)/shard_map/psum | solution.py:117
  513.2 2.2 multiply_reduce_fusion
  516.1 2.7 collective-permute-start
  518.8 22.3 %collective-permute-done = f32[1,64,4096]{2,1,0:T(8,128)S(1)} collective-permute-done((f32[1,64,4096]{2,1,0:T(8,128)S(1)}, f32[1,64,4096]{2,1,0:T(8,128)S(1)}, u32[]{:S(2)}, u32[]{:S(2)}) %collective-permute-start) | collective-permute-done | bytes 1048608 | tf_op jit(solution)/shard_map/ppermute | solution.py:16
  542.2 74.8 %all-gather.10.cloned.1.call-done = bf16[1,1024,4096]{2,1,0:T(8,128)(2,1)} async-done(((bf16[1,64,4096]{2,1,0:T(8,128)(2,1)}), bf16[1,1024,4096]{2,1,0:T(8,128)(2,1)}) %all-gather.10.cloned.1.call-update) | async-done | bytes 8388624 | tf_op jit(solution)/shard_map/all_gather | solution.py:123
  617.1 12.6 %fusion = f32[1024,1024]{1,0:T(8,128)S(1)} fusion(bf16[4096,1024]{1,0:T(8,128)(2,1)} %param.24, bf16[1,1024,4096]{2,1,0:T(8,128)(2,1)} %all-gather.10.cloned.1.call-done), kind=kOutput, calls=%fused_computation.2 | convolution fusion | flops 8589934592 | bytes 20971520 | tf_op jit(solution)/shard_map/dot_general | solution.py:122
  629.7 2.0 copy-done.3
  631.7 2.2 copy.39
  633.9 2.5 reduce_max.31
  636.5 64.1 %pmax.7 = f32[1024]{0:T(1024)S(1)} all-reduce(f32[1024]{0:T(1024)S(1)} %reduce_max.32), channel_id=1, replica_groups=mesh['wide'=16,'narrow'=8] {'wide','narrow'}, use_global_device_ids=true, to_apply=%region_10.11 | all-reduce | flops 1024 | bytes 8192 | tf_op jit(solution)/shard_map/pmax | solution.py:130
  700.6 2.9 exponential_reduce_fusion
  703.6 62.5 %psum.15 = f32[1024]{0:T(1024)S(1)} all-reduce(f32[1024]{0:T(1024)S(1)} %reduce_sum.72), channel_id=1, replica_groups=mesh['wide'=16,'narrow'=8] {'wide','narrow'}, use_global_device_ids=true, to_apply=%region_12.13 | all-reduce | flops 1024 | bytes 8192 | tf_op jit(solution)/shard_map/psum | solution.py:131
  766.8 4.7 bitcast_subtract_fusion
  (63 shorter events, 12.5 us)
Async XLA Ops:
  7.2 1.6 copy-start
  7.2 2.8 copy-start.12
  7.2 40.9 %all-gather.6.cloned.1.call-start = ((), (), s32[]{:S(2)}) async-start(), calls=%async_computation | async-start | bytes 1179648 | tf_op jit(solution)/shard_map/all_gather | solution.py:62
  7.9 386.1 %all-gather.8.cloned.1.call-start = ((), (), s32[]{:S(2)}) async-start(), calls=%async_computation.2 | async-start | bytes 18874368 | tf_op jit(solution)/shard_map/all_gather | solution.py:108
  8.8 40.8 %copy-start.9 = (f32[4096]{0:T(1024)S(1)}, f32[4096]{0:T(1024)}, u32[]{:S(2)}) copy-start(f32[4096]{0:T(1024)} %param.15) | copy-start | bytes 49156
  55.0 2.8 copy-start.6
  59.7 2.2 copy-start.7
  64.0 1.2 copy-start.2
  64.0 449.1 %all-reduce.2.cloned.1.call-start = ((), (), s32[]{:S(2)}) async-start(), calls=%async_computation.1 | async-start | bytes 4194304 | tf_op jit(solution)/shard_map/psum | solution.py:117
  401.4 0.7 copy-start.10
  402.1 1.4 copy-start.8
  402.6 1.0 copy-start.4
  408.0 209.1 %all-gather.10.cloned.1.call-start = ((), (), s32[]{:S(2)}) async-start(), calls=%async_computation.3 | async-start | bytes 8912896 | tf_op jit(solution)/shard_map/all_gather | solution.py:123
  408.0 107.4 %copy-start.11 = (f32[4096]{0:T(1024)S(1)}, f32[4096]{0:T(1024)}, u32[]{:S(2)}) copy-start(f32[4096]{0:T(1024)} %param.17) | copy-start | bytes 49156
  513.2 2.2 copy-start.5
  516.1 25.1 %collective-permute-start = (f32[1,64,4096]{2,1,0:T(8,128)S(1)}, f32[1,64,4096]{2,1,0:T(8,128)S(1)}, u32[]{:S(2)}, u32[]{:S(2)}) collective-permute-start(f32[1,64,4096]{2,1,0:T(8,128)S(1)} %slice_select_fusion), channel_id=1, source_target_pairs={{0,64},{8,72},{16,80},{24,88},{32,96},{40,104},{48,112},{56,120},{... | collective-permute-start | bytes 3145736 | tf_op jit(solution)/shard_map/ppermute | solution.py:16
  629.7 2.0 copy-start.3
  766.8 4.7 copy-start.1
Sparse Core Ops, SparseCore 0:
  9.6 38.3 all-gather.5
  64.1 329.8 all-gather.7
  408.1 105.0 all-reduce.1
  542.4 74.6 all-gather.9
